TPU v7x, 32 devices: a whole 2x2x4 slice. The times are simulated.
32 devices in a mesh: blk: 16 (over z, y, x), col: 2 (over core).
Axes of the slice: x: 2, y: 2, z: 4, core: 2. Of those that a mesh axis runs over, the one named last changes fastest.
Arguments:
- queries: bfloat16 [128, 16384], P('blk', 'col'), may hold values from -6 to 6
- factor: bfloat16 [16384, 1024], P('col', 'blk'), may hold values from -0.046875 to 0.046875
- eigenvalues: float32 [1024], replicated, may hold values from 0.05 to 20
- damping: float32 [1], replicated, may hold values from 0.5 to 2
- train_rows: bfloat16 [16384, 16384], P('blk', 'col'), may hold values from -0.046875 to 0.046875
Outputs:
- scores: bfloat16 [128, 16384], P('col', 'blk')
All inputs are finite; a program needn't handle non-finite values.
Results may differ from a plain program's by a relative error of at most 0.0049.
Values may be sent and summed in bfloat16 or wider, within the bound.
A program may use at most 64 MiB of HBM per device.

v0:
```python
import jax
import jax.numpy as jnp
from jax import lax
from jax.sharding import PartitionSpec as P


def per_device(queries, factor, eigenvalues, damping, train_rows):
    damp_value = damping[0]
    weights = eigenvalues / (eigenvalues + damp_value)
    query_part = lax.all_to_all(queries, "blk", split_axis=1, concat_axis=0, tiled=True)
    factor_part = lax.all_to_all(factor, "blk", split_axis=0, concat_axis=1, tiled=True)
    partial_value = jnp.dot(query_part, factor_part, preferred_element_type=jnp.float32)
    coefficient = lax.psum(partial_value, ("blk", "col"))
    scaled = coefficient * weights[None, :]
    correction = jnp.dot(scaled, factor_part.astype(jnp.float32).T, precision=lax.Precision.HIGHEST)
    pre_part = ((query_part.astype(jnp.float32) - correction) / damp_value).astype(jnp.bfloat16)
    pre_all = lax.all_gather(pre_part, "blk", axis=1, tiled=True)
    partial_scores = jnp.einsum(
        "qk,nk->qn", pre_all, train_rows, preferred_element_type=jnp.float32
    )
    scores = lax.psum_scatter(partial_scores, "col", scatter_dimension=0, tiled=True)
    return scores.astype(jnp.bfloat16)


def solution(mesh):
    in_specs = (P("blk", "col"), P("col", "blk"), P(), P(), P("blk", "col"))
    out_specs = P("col", "blk")
    return jax.shard_map(
        per_device, mesh=mesh, in_specs=in_specs, out_specs=out_specs, check_vma=False
    )
```

profile of v0, /device:TPU:0, one launch (start us, length us, event | category | flops | bytes accessed | tf_op | source)
XLA Modules:
  0.0 269.8 jit_solution(12998497539709083565)
XLA Ops:
  6.5 8.3 %all-to-all-start = ((bf16[8,16,512]{2,0,1:T(8,128)(2,1)}), bf16[8,16,512]{2,0,1:T(8,128)(2,1)S(1)}, u32[]{:S(2)}, u32[]{:S(2)}) async-start(bf16[8,16,512]{2,0,1:T(8,128)(2,1)} %bitcast.25), calls=%async_computation | async-start | bytes 262144 | tf_op jit(solution)/shard_map/all_to_all | solution.py:10
  14.9 0.0 all-reduce.2.cloned.1.call-start
  14.9 1.3 copy.10
  16.3 6.4 %all-to-all-done = bf16[8,16,512]{2,0,1:T(8,128)(2,1)S(1)} async-done(((bf16[8,16,512]{2,0,1:T(8,128)(2,1)}), bf16[8,16,512]{2,0,1:T(8,128)(2,1)S(1)}, u32[]{:S(2)}, u32[]{:S(2)}) %all-to-all-start) | async-done | bytes 131104 | tf_op jit(solution)/shard_map/all_to_all | solution.py:10
  22.7 28.3 %all_to_all.38 = bf16[16,512,64]{1,2,0:T(8,128)(2,1)S(1)} all-to-all(bf16[16,512,64]{1,2,0:T(8,128)(2,1)S(1)} %bitcast.21), channel_id=1, replica_groups=mesh['blk'=16,'col'=2] {'blk'}, dimensions={0} | all-to-all | bytes 2097152 | tf_op jit(solution)/shard_map/all_to_all | solution.py:11
  51.0 1.3 fusion.4
  52.3 0.0 all-reduce.2.cloned.1.call-update
  52.3 0.0 all-gather.2.cloned.1.call-start
  53.0 0.7 add_divide_fusion
  53.7 126.2 %all-reduce.2.cloned.1.call-done = f32[128,1024]{1,0:T(8,128)} async-done(((f32[128,1024]{1,0:T(8,128)}), f32[128,1024]{1,0:T(8,128)}) %all-reduce.2.cloned.1.call-update) | async-done | bytes 524304 | tf_op jit(solution)/shard_map/psum | solution.py:13
  179.9 2.3 fusion.1
  182.2 0.0 all-gather.2.cloned.1.call-update
  182.2 0.0 reduce-scatter.2.cloned.1.call-start
  182.2 60.3 %all-gather.2.cloned.1.call-done = bf16[128,8192]{1,0:T(8,128)(2,1)} async-done(((bf16[128,512]{1,0:T(8,128)(2,1)}), bf16[128,8192]{1,0:T(8,128)(2,1)}) %all-gather.2.cloned.1.call-update) | async-done | bytes 2097168 | tf_op jit(solution)/shard_map/all_gather | solution.py:17
  242.5 12.9 %fusion.6 = f32[128,1024]{1,0:T(8,128)} fusion(bf16[128,8192]{1,0:T(8,128)(2,1)} %all-gather.2.cloned.1.call-done, bf16[1024,8192]{1,0:T(8,128)(2,1)} %param.9), kind=kOutput, calls=%fused_computation.9 | convolution fusion | flops 2147483648 | bytes 19398656 | tf_op jit(solution)/shard_map/qk,nk->qn/dot_general | solution.py:18
  255.4 0.0 reduce-scatter.2.cloned.1.call-update
  255.4 6.3 %reduce-scatter.2.cloned.1.call-done = f32[64,1024]{1,0:T(8,128)} async-done(((f32[128,1024]{1,0:T(8,128)}), f32[64,1024]{1,0:T(8,128)}) %reduce-scatter.2.cloned.1.call-update) | async-done | bytes 262160 | tf_op jit(solution)/shard_map/reduce_scatter | solution.py:21
  261.7 1.6 convert_element_type.12
Async XLA Ops:
  6.5 16.1 %all-to-all-start = ((bf16[8,16,512]{2,0,1:T(8,128)(2,1)}), bf16[8,16,512]{2,0,1:T(8,128)(2,1)S(1)}, u32[]{:S(2)}, u32[]{:S(2)}) async-start(bf16[8,16,512]{2,0,1:T(8,128)(2,1)} %bitcast.25), calls=%async_computation | async-start | bytes 262144 | tf_op jit(solution)/shard_map/all_to_all | solution.py:10
  14.9 165.0 %all-reduce.2.cloned.1.call-start = ((), (), s32[]{:S(2)}) async-start(), calls=%async_computation.3 | async-start | bytes 1048576 | tf_op jit(solution)/shard_map/psum | solution.py:13
  52.3 190.2 %all-gather.2.cloned.1.call-start = ((), (), s32[]{:S(2)}) async-start(), calls=%async_computation.4 | async-start | bytes 2228224 | tf_op jit(solution)/shard_map/all_gather | solution.py:17
  182.2 79.5 %reduce-scatter.2.cloned.1.call-start = ((), (), s32[]{:S(2)}) async-start(), calls=%async_computation.5 | async-start | bytes 786432 | tf_op jit(solution)/shard_map/reduce_scatter | solution.py:21
Sparse Core Ops, SparseCore 0:
  52.4 127.3 all-reduce.1
  182.6 59.8 all-gather.1
  255.6 6.0 reduce-scatter.1
where the time goes:
time: 270 us
  waiting for transfers between devices  199 us (74%)
  blocking collectives  28.3 us (10%)
  matrix products  16.4 us (6%)
  between operations  13.8 us (5%)
  starting transfers between devices  8.47 us (3%)
    psum x1, waiting for transfers between devices, per_device(): coefficient = lax.psum(partial_value, ('blk', 'col'))  126 us
    all_gather x1, waiting for transfers between devices, per_device(): pre_all = lax.all_gather(pre_part, 'blk', axis=1, tiled=True)  60.3 us
    all_to_all x1, blocking collectives, per_device(): lax.all_to_all(factor, 'blk', split_axis=0, concat_axis=1, tiled=True)  28.3 us
    dot_general x1, matrix products, per_device(): jnp.einsum('qk,nk->qn', pre_all, train_rows, preferred_element_type=jnp.f...  12.9 us
    all_to_all x1, starting transfers between devices, per_device(): lax.all_to_all(queries, 'blk', split_axis=1, concat_axis=0, tiled=True)  8.34 us
    all_to_all x1, waiting for transfers between devices, per_device(): lax.all_to_all(queries, 'blk', split_axis=1, concat_axis=0, tiled=True)  6.41 us
    reduce_scatter x1, waiting for transfers between devices, per_device(): lax.psum_scatter(partial_scores, 'col', scatter_dimension=0, tiled=True)  6.26 us
  transfers between devices with their start and end apart: 4, of which 4 were waited for; matrix products, arithmetic and copies ran while one was open for 1% of the time, Pallas kernels for 0%

commit v1 on v0

--- a/solution.py
+++ b/solution.py
@@ -2,6 +2,18 @@
 import jax.numpy as jnp
 from jax import lax
 from jax.sharding import PartitionSpec as P
+
+
+def summed_around(x, axis, dim, term):
+    size, mine = (lax.axis_size(axis), lax.axis_index(axis))
+    downward = [(i, (i - 1) % size) for i in range(size)]
+    rows = x.shape[dim]
+    current = x
+    running = term(current, mine * rows)
+    for hop in range(1, size):
+        current = lax.ppermute(current, axis, downward)
+        running = running + term(current, (mine + hop) % size * rows)
+    return running
 
 
 def per_device(queries, factor, eigenvalues, damping, train_rows):
@@ -14,9 +26,16 @@
     scaled = coefficient * weights[None, :]
     correction = jnp.dot(scaled, factor_part.astype(jnp.float32).T, precision=lax.Precision.HIGHEST)
     pre_part = ((query_part.astype(jnp.float32) - correction) / damp_value).astype(jnp.bfloat16)
-    pre_all = lax.all_gather(pre_part, "blk", axis=1, tiled=True)
-    partial_scores = jnp.einsum(
-        "qk,nk->qn", pre_all, train_rows, preferred_element_type=jnp.float32
+    partial_scores = summed_around(
+        pre_part,
+        "blk",
+        1,
+        lambda part, at: jnp.einsum(
+            "qk,nk->qn",
+            part,
+            lax.dynamic_slice_in_dim(train_rows, at, part.shape[1], axis=1),
+            preferred_element_type=jnp.float32,
+        ),
     )
     scores = lax.psum_scatter(partial_scores, "col", scatter_dimension=0, tiled=True)
     return scores.astype(jnp.bfloat16)

time: 270 us -> 331 us (1.23)
  starting transfers between devices: 8.47 us -> 96.5 us
  waiting for transfers between devices: 199 us -> 168 us
  matrix products: 16.4 us -> 20.1 us
    ppermute x0 -> x15, starting transfers between devices: none -> 88 us  [summed_around(): current = lax.ppermute(current, axis, downward)]
    all_gather x1 -> x0, waiting for transfers between devices: 60.3 us -> none  [per_device(): pre_all = lax.all_gather(pre_part, 'blk', axis=1, tiled=True)]
    ppermute x0 -> x15, waiting for transfers between devices: none -> 25.4 us  [summed_around(): current = lax.ppermute(current, axis, downward)]
    dot_general x1 -> x16, matrix products: 12.9 us -> 17 us  [per_device(): jnp.einsum('qk,nk->qn', part, lax.dynamic_slice_in_dim(train_rows, at, pa...]
    reduce_scatter x1, waiting for transfers between devices: 6.26 us -> 9.9 us  [per_device(): lax.psum_scatter(partial_scores, 'col', scatter_dimension=0, tiled=True)]
  transfers between devices with their start and end apart: 4 -> 18, of which waited for: 4 -> 18; matrix products, arithmetic and copies ran while one was open for 1% -> 5% of each run, Pallas kernels for 0% -> 0%
where the time goes in v1:
time: 331 us
  waiting for transfers between devices  168 us (51%)
  starting transfers between devices  96.5 us (29%)
  blocking collectives  28.3 us (9%)
  matrix products  20.1 us (6%)
  between operations  14.4 us (4%)
    psum x1, waiting for transfers between devices, per_device(): coefficient = lax.psum(partial_value, ('blk', 'col'))  126 us
    ppermute x15, starting transfers between devices, summed_around(): current = lax.ppermute(current, axis, downward)  88 us
    all_to_all x1, blocking collectives, per_device(): lax.all_to_all(factor, 'blk', split_axis=0, concat_axis=1, tiled=True)  28.3 us
    ppermute x15, waiting for transfers between devices, summed_around(): current = lax.ppermute(current, axis, downward)  25.4 us
    dot_general x16, matrix products, per_device(): jnp.einsum('qk,nk->qn', part, lax.dynamic_slice_in_dim(train_rows, at, pa...  17 us
    reduce_scatter x1, waiting for transfers between devices, per_device(): lax.psum_scatter(partial_scores, 'col', scatter_dimension=0, tiled=True)  9.9 us
    all_to_all x1, starting transfers between devices, per_device(): lax.all_to_all(queries, 'blk', split_axis=1, concat_axis=0, tiled=True)  8.34 us
  transfers between devices with their start and end apart: 18, of which 18 were waited for; matrix products, arithmetic and copies ran while one was open for 5% of the time, Pallas kernels for 0%

profile of v1, /device:TPU:0, one launch (start us, length us, event | category | flops | bytes accessed | tf_op | source)
XLA Modules:
  0.0 330.7 jit_solution(13616123613609775824)
XLA Ops:
  6.5 8.3 %all-to-all-start = ((bf16[8,16,512]{2,0,1:T(8,128)(2,1)}), bf16[8,16,512]{2,0,1:T(8,128)(2,1)S(1)}, u32[]{:S(2)}, u32[]{:S(2)}) async-start(bf16[8,16,512]{2,0,1:T(8,128)(2,1)} %bitcast.39), calls=%async_computation | async-start | bytes 262144 | tf_op jit(solution)/shard_map/all_to_all | solution.py:22
  14.9 0.0 all-reduce.2.cloned.1.call-start
  14.9 1.3 copy.10
  16.3 6.4 %all-to-all-done = bf16[8,16,512]{2,0,1:T(8,128)(2,1)S(1)} async-done(((bf16[8,16,512]{2,0,1:T(8,128)(2,1)}), bf16[8,16,512]{2,0,1:T(8,128)(2,1)S(1)}, u32[]{:S(2)}, u32[]{:S(2)}) %all-to-all-start) | async-done | bytes 131104 | tf_op jit(solution)/shard_map/all_to_all | solution.py:22
  22.7 28.3 %all_to_all.38 = bf16[16,512,64]{1,2,0:T(8,128)(2,1)S(1)} all-to-all(bf16[16,512,64]{1,2,0:T(8,128)(2,1)S(1)} %bitcast.35), channel_id=1, replica_groups=mesh['blk'=16,'col'=2] {'blk'}, dimensions={0} | all-to-all | bytes 2097152 | tf_op jit(solution)/shard_map/all_to_all | solution.py:23
  51.0 1.3 fusion.21
  52.3 0.0 all-reduce.2.cloned.1.call-update
  52.3 0.0 reduce-scatter.2.cloned.1.call-start
  53.2 0.7 add_divide_fusion
  53.9 126.0 %all-reduce.2.cloned.1.call-done = f32[128,1024]{1,0:T(8,128)} async-done(((f32[128,1024]{1,0:T(8,128)}), f32[128,1024]{1,0:T(8,128)}) %all-reduce.2.cloned.1.call-update) | async-done | bytes 524304 | tf_op jit(solution)/shard_map/psum | solution.py:25
  179.9 0.0 copy-start
  179.9 1.8 fusion.1
  181.7 3.3 collective-permute-start
  185.0 1.7 fusion.17
  186.7 0.8 collective-permute-done
  187.5 6.0 %collective-permute-start.1 = (bf16[128,512]{1,0:T(8,128)(2,1)S(1)}, bf16[128,512]{1,0:T(8,128)(2,1)S(1)}, u32[]{:S(2)}, u32[]{:S(2)}) collective-permute-start(bf16[128,512]{1,0:T(8,128)(2,1)S(1)} %collective-permute-done), channel_id=1, source_target_pairs={{0,30},{2,0},{4,2},{6,4},{8,6},{10,8},{12,10},{14,12},{16,14},{18,... | collective-permute-start | bytes 393224 | tf_op jit(solution)/shard_map/ppermute | solution.py:14
  193.5 1.7 convolution_add_fusion.14
  195.2 0.8 collective-permute-done.1
  196.1 6.0 %collective-permute-start.2 = (bf16[128,512]{1,0:T(8,128)(2,1)S(1)}, bf16[128,512]{1,0:T(8,128)(2,1)S(1)}, u32[]{:S(2)}, u32[]{:S(2)}) collective-permute-start(bf16[128,512]{1,0:T(8,128)(2,1)S(1)} %collective-permute-done.1), channel_id=1, source_target_pairs={{0,30},{2,0},{4,2},{6,4},{8,6},{10,8},{12,10},{14,12},{16,14},{18,... | collective-permute-start | bytes 393224 | tf_op jit(solution)/shard_map/ppermute | solution.py:14
  202.1 1.7 convolution_add_fusion.13
  203.8 0.8 collective-permute-done.2
  204.6 6.0 %collective-permute-start.3 = (bf16[128,512]{1,0:T(8,128)(2,1)S(1)}, bf16[128,512]{1,0:T(8,128)(2,1)S(1)}, u32[]{:S(2)}, u32[]{:S(2)}) collective-permute-start(bf16[128,512]{1,0:T(8,128)(2,1)S(1)} %collective-permute-done.2), channel_id=1, source_target_pairs={{0,30},{2,0},{4,2},{6,4},{8,6},{10,8},{12,10},{14,12},{16,14},{18,... | collective-permute-start | bytes 393224 | tf_op jit(solution)/shard_map/ppermute | solution.py:14
  210.7 1.7 convolution_add_fusion.12
  212.4 0.8 collective-permute-done.3
  213.2 6.0 %collective-permute-start.4 = (bf16[128,512]{1,0:T(8,128)(2,1)S(1)}, bf16[128,512]{1,0:T(8,128)(2,1)S(1)}, u32[]{:S(2)}, u32[]{:S(2)}) collective-permute-start(bf16[128,512]{1,0:T(8,128)(2,1)S(1)} %collective-permute-done.3), channel_id=1, source_target_pairs={{0,30},{2,0},{4,2},{6,4},{8,6},{10,8},{12,10},{14,12},{16,14},{18,... | collective-permute-start | bytes 393224 | tf_op jit(solution)/shard_map/ppermute | solution.py:14
  219.2 1.7 convolution_add_fusion.11
  220.9 1.3 collective-permute-done.4
  222.2 6.1 %collective-permute-start.5 = (bf16[128,512]{1,0:T(8,128)(2,1)S(1)}, bf16[128,512]{1,0:T(8,128)(2,1)S(1)}, u32[]{:S(2)}, u32[]{:S(2)}) collective-permute-start(bf16[128,512]{1,0:T(8,128)(2,1)S(1)} %collective-permute-done.4), channel_id=1, source_target_pairs={{0,30},{2,0},{4,2},{6,4},{8,6},{10,8},{12,10},{14,12},{16,14},{18,... | collective-permute-start | bytes 393224 | tf_op jit(solution)/shard_map/ppermute | solution.py:14
  228.3 1.7 convolution_add_fusion.10
  230.0 1.9 collective-permute-done.5
  231.9 6.1 %collective-permute-start.6 = (bf16[128,512]{1,0:T(8,128)(2,1)S(1)}, bf16[128,512]{1,0:T(8,128)(2,1)S(1)}, u32[]{:S(2)}, u32[]{:S(2)}) collective-permute-start(bf16[128,512]{1,0:T(8,128)(2,1)S(1)} %collective-permute-done.5), channel_id=1, source_target_pairs={{0,30},{2,0},{4,2},{6,4},{8,6},{10,8},{12,10},{14,12},{16,14},{18,... | collective-permute-start | bytes 393224 | tf_op jit(solution)/shard_map/ppermute | solution.py:14
  238.0 1.7 convolution_add_fusion.9
  239.7 1.1 collective-permute-done.6
  240.8 6.1 %collective-permute-start.7 = (bf16[128,512]{1,0:T(8,128)(2,1)S(1)}, bf16[128,512]{1,0:T(8,128)(2,1)S(1)}, u32[]{:S(2)}, u32[]{:S(2)}) collective-permute-start(bf16[128,512]{1,0:T(8,128)(2,1)S(1)} %collective-permute-done.6), channel_id=1, source_target_pairs={{0,30},{2,0},{4,2},{6,4},{8,6},{10,8},{12,10},{14,12},{16,14},{18,... | collective-permute-start | bytes 393224 | tf_op jit(solution)/shard_map/ppermute | solution.py:14
  246.9 0.0 copy-done
  246.9 0.5 convolution_add_fusion.8
  247.4 2.0 collective-permute-done.7
  249.4 6.0 %collective-permute-start.8 = (bf16[128,512]{1,0:T(8,128)(2,1)S(1)}, bf16[128,512]{1,0:T(8,128)(2,1)S(1)}, u32[]{:S(2)}, u32[]{:S(2)}) collective-permute-start(bf16[128,512]{1,0:T(8,128)(2,1)S(1)} %collective-permute-done.7), channel_id=1, source_target_pairs={{0,30},{2,0},{4,2},{6,4},{8,6},{10,8},{12,10},{14,12},{16,14},{18,... | collective-permute-start | bytes 393224 | tf_op jit(solution)/shard_map/ppermute | solution.py:14
  255.4 0.5 convolution_add_fusion.7
  255.9 2.0 collective-permute-done.8
  257.9 6.0 %collective-permute-start.9 = (bf16[128,512]{1,0:T(8,128)(2,1)S(1)}, bf16[128,512]{1,0:T(8,128)(2,1)S(1)}, u32[]{:S(2)}, u32[]{:S(2)}) collective-permute-start(bf16[128,512]{1,0:T(8,128)(2,1)S(1)} %collective-permute-done.8), channel_id=1, source_target_pairs={{0,30},{2,0},{4,2},{6,4},{8,6},{10,8},{12,10},{14,12},{16,14},{18,... | collective-permute-start | bytes 393224 | tf_op jit(solution)/shard_map/ppermute | solution.py:14
  264.0 0.5 convolution_add_fusion.6
  264.5 2.0 collective-permute-done.9
  266.5 6.0 %collective-permute-start.10 = (bf16[128,512]{1,0:T(8,128)(2,1)S(1)}, bf16[128,512]{1,0:T(8,128)(2,1)S(1)}, u32[]{:S(2)}, u32[]{:S(2)}) collective-permute-start(bf16[128,512]{1,0:T(8,128)(2,1)S(1)} %collective-permute-done.9), channel_id=1, source_target_pairs={{0,30},{2,0},{4,2},{6,4},{8,6},{10,8},{12,10},{14,12},{16,14},{18,... | collective-permute-start | bytes 393224 | tf_op jit(solution)/shard_map/ppermute | solution.py:14
  272.5 0.5 convolution_add_fusion.5
  273.0 2.0 collective-permute-done.10
  275.1 6.0 %collective-permute-start.11 = (bf16[128,512]{1,0:T(8,128)(2,1)S(1)}, bf16[128,512]{1,0:T(8,128)(2,1)S(1)}, u32[]{:S(2)}, u32[]{:S(2)}) collective-permute-start(bf16[128,512]{1,0:T(8,128)(2,1)S(1)} %collective-permute-done.10), channel_id=1, source_target_pairs={{0,30},{2,0},{4,2},{6,4},{8,6},{10,8},{12,10},{14,12},{16,14},{18,... | collective-permute-start | bytes 393224 | tf_op jit(solution)/shard_map/ppermute | solution.py:14
  281.1 0.5 convolution_add_fusion.4
  281.6 2.6 collective-permute-done.11
  284.2 6.1 %collective-permute-start.12 = (bf16[128,512]{1,0:T(8,128)(2,1)S(1)}, bf16[128,512]{1,0:T(8,128)(2,1)S(1)}, u32[]{:S(2)}, u32[]{:S(2)}) collective-permute-start(bf16[128,512]{1,0:T(8,128)(2,1)S(1)} %collective-permute-done.11), channel_id=1, source_target_pairs={{0,30},{2,0},{4,2},{6,4},{8,6},{10,8},{12,10},{14,12},{16,14},{18,... | collective-permute-start | bytes 393224 | tf_op jit(solution)/shard_map/ppermute | solution.py:14
  290.2 0.5 convolution_add_fusion.3
  290.7 3.1 collective-permute-done.12
  293.8 6.1 %collective-permute-start.13 = (bf16[128,512]{1,0:T(8,128)(2,1)S(1)}, bf16[128,512]{1,0:T(8,128)(2,1)S(1)}, u32[]{:S(2)}, u32[]{:S(2)}) collective-permute-start(bf16[128,512]{1,0:T(8,128)(2,1)S(1)} %collective-permute-done.12), channel_id=1, source_target_pairs={{0,30},{2,0},{4,2},{6,4},{8,6},{10,8},{12,10},{14,12},{16,14},{18,... | collective-permute-start | bytes 393224 | tf_op jit(solution)/shard_map/ppermute | solution.py:14
  299.9 0.5 convolution_add_fusion.2
  300.4 2.0 collective-permute-done.13
  302.4 6.0 %collective-permute-start.14 = (bf16[128,512]{1,0:T(8,128)(2,1)S(1)}, bf16[128,512]{1,0:T(8,128)(2,1)S(1)}, u32[]{:S(2)}, u32[]{:S(2)}) collective-permute-start(bf16[128,512]{1,0:T(8,128)(2,1)S(1)} %collective-permute-done.13), channel_id=1, source_target_pairs={{0,30},{2,0},{4,2},{6,4},{8,6},{10,8},{12,10},{14,12},{16,14},{18,... | collective-permute-start | bytes 393224 | tf_op jit(solution)/shard_map/ppermute | solution.py:14
  308.5 0.5 convolution_add_fusion.1
  309.0 2.0 collective-permute-done.14
  311.0 1.3 convolution_add_fusion
  312.3 0.0 reduce-scatter.2.cloned.1.call-update
  312.3 9.9 %reduce-scatter.2.cloned.1.call-done = f32[64,1024]{1,0:T(8,128)} async-done(((f32[128,1024]{1,0:T(8,128)}), f32[64,1024]{1,0:T(8,128)}) %reduce-scatter.2.cloned.1.call-update) | async-done | bytes 262160 | tf_op jit(solution)/shard_map/reduce_scatter | solution.py:40
  322.2 1.6 convert_element_type.12
Async XLA Ops:
  6.5 16.1 %all-to-all-start = ((bf16[8,16,512]{2,0,1:T(8,128)(2,1)}), bf16[8,16,512]{2,0,1:T(8,128)(2,1)S(1)}, u32[]{:S(2)}, u32[]{:S(2)}) async-start(bf16[8,16,512]{2,0,1:T(8,128)(2,1)} %bitcast.39), calls=%async_computation | async-start | bytes 262144 | tf_op jit(solution)/shard_map/all_to_all | solution.py:22
  14.9 165.0 %all-reduce.2.cloned.1.call-start = ((), (), s32[]{:S(2)}) async-start(), calls=%async_computation.3 | async-start | bytes 1048576 | tf_op jit(solution)/shard_map/psum | solution.py:25
  52.3 269.9 %reduce-scatter.2.cloned.1.call-start = ((), (), s32[]{:S(2)}) async-start(), calls=%async_computation.4 | async-start | bytes 786432 | tf_op jit(solution)/shard_map/reduce_scatter | solution.py:40
  179.9 67.0 %copy-start = (bf16[1024,8192]{1,0:T(8,128)(2,1)S(1)}, bf16[1024,8192]{1,0:T(8,128)(2,1)}, u32[]{:S(2)}) copy-start(bf16[1024,8192]{1,0:T(8,128)(2,1)} %param.9) | copy-start | bytes 50331652
  181.7 5.8 %collective-permute-start = (bf16[128,512]{1,0:T(8,128)(2,1)S(1)}, bf16[128,512]{1,0:T(8,128)(2,1)S(1)}, u32[]{:S(2)}, u32[]{:S(2)}) collective-permute-start(bf16[128,512]{1,0:T(8,128)(2,1)S(1)} %fusion.1), channel_id=1, source_target_pairs={{0,30},{2,0},{4,2},{6,4},{8,6},{10,8},{12,10},{14,12},{16,14},{18,... | collective-permute-start | bytes 393224 | tf_op jit(solution)/shard_map/ppermute | solution.py:14
  187.5 8.6 %collective-permute-start.1 = (bf16[128,512]{1,0:T(8,128)(2,1)S(1)}, bf16[128,512]{1,0:T(8,128)(2,1)S(1)}, u32[]{:S(2)}, u32[]{:S(2)}) collective-permute-start(bf16[128,512]{1,0:T(8,128)(2,1)S(1)} %collective-permute-done), channel_id=1, source_target_pairs={{0,30},{2,0},{4,2},{6,4},{8,6},{10,8},{12,10},{14,12},{16,14},{18,... | collective-permute-start | bytes 393224 | tf_op jit(solution)/shard_map/ppermute | solution.py:14
  196.1 8.6 %collective-permute-start.2 = (bf16[128,512]{1,0:T(8,128)(2,1)S(1)}, bf16[128,512]{1,0:T(8,128)(2,1)S(1)}, u32[]{:S(2)}, u32[]{:S(2)}) collective-permute-start(bf16[128,512]{1,0:T(8,128)(2,1)S(1)} %collective-permute-done.1), channel_id=1, source_target_pairs={{0,30},{2,0},{4,2},{6,4},{8,6},{10,8},{12,10},{14,12},{16,14},{18,... | collective-permute-start | bytes 393224 | tf_op jit(solution)/shard_map/ppermute | solution.py:14
  204.6 8.6 %collective-permute-start.3 = (bf16[128,512]{1,0:T(8,128)(2,1)S(1)}, bf16[128,512]{1,0:T(8,128)(2,1)S(1)}, u32[]{:S(2)}, u32[]{:S(2)}) collective-permute-start(bf16[128,512]{1,0:T(8,128)(2,1)S(1)} %collective-permute-done.2), channel_id=1, source_target_pairs={{0,30},{2,0},{4,2},{6,4},{8,6},{10,8},{12,10},{14,12},{16,14},{18,... | collective-permute-start | bytes 393224 | tf_op jit(solution)/shard_map/ppermute | solution.py:14
  213.2 9.0 %collective-permute-start.4 = (bf16[128,512]{1,0:T(8,128)(2,1)S(1)}, bf16[128,512]{1,0:T(8,128)(2,1)S(1)}, u32[]{:S(2)}, u32[]{:S(2)}) collective-permute-start(bf16[128,512]{1,0:T(8,128)(2,1)S(1)} %collective-permute-done.3), channel_id=1, source_target_pairs={{0,30},{2,0},{4,2},{6,4},{8,6},{10,8},{12,10},{14,12},{16,14},{18,... | collective-permute-start | bytes 393224 | tf_op jit(solution)/shard_map/ppermute | solution.py:14
  222.2 9.7 %collective-permute-start.5 = (bf16[128,512]{1,0:T(8,128)(2,1)S(1)}, bf16[128,512]{1,0:T(8,128)(2,1)S(1)}, u32[]{:S(2)}, u32[]{:S(2)}) collective-permute-start(bf16[128,512]{1,0:T(8,128)(2,1)S(1)} %collective-permute-done.4), channel_id=1, source_target_pairs={{0,30},{2,0},{4,2},{6,4},{8,6},{10,8},{12,10},{14,12},{16,14},{18,... | collective-permute-start | bytes 393224 | tf_op jit(solution)/shard_map/ppermute | solution.py:14
  231.9 8.8 %collective-permute-start.6 = (bf16[128,512]{1,0:T(8,128)(2,1)S(1)}, bf16[128,512]{1,0:T(8,128)(2,1)S(1)}, u32[]{:S(2)}, u32[]{:S(2)}) collective-permute-start(bf16[128,512]{1,0:T(8,128)(2,1)S(1)} %collective-permute-done.5), channel_id=1, source_target_pairs={{0,30},{2,0},{4,2},{6,4},{8,6},{10,8},{12,10},{14,12},{16,14},{18,... | collective-permute-start | bytes 393224 | tf_op jit(solution)/shard_map/ppermute | solution.py:14
  240.8 8.6 %collective-permute-start.7 = (bf16[128,512]{1,0:T(8,128)(2,1)S(1)}, bf16[128,512]{1,0:T(8,128)(2,1)S(1)}, u32[]{:S(2)}, u32[]{:S(2)}) collective-permute-start(bf16[128,512]{1,0:T(8,128)(2,1)S(1)} %collective-permute-done.6), channel_id=1, source_target_pairs={{0,30},{2,0},{4,2},{6,4},{8,6},{10,8},{12,10},{14,12},{16,14},{18,... | collective-permute-start | bytes 393224 | tf_op jit(solution)/shard_map/ppermute | solution.py:14
  249.4 8.6 %collective-permute-start.8 = (bf16[128,512]{1,0:T(8,128)(2,1)S(1)}, bf16[128,512]{1,0:T(8,128)(2,1)S(1)}, u32[]{:S(2)}, u32[]{:S(2)}) collective-permute-start(bf16[128,512]{1,0:T(8,128)(2,1)S(1)} %collective-permute-done.7), channel_id=1, source_target_pairs={{0,30},{2,0},{4,2},{6,4},{8,6},{10,8},{12,10},{14,12},{16,14},{18,... | collective-permute-start | bytes 393224 | tf_op jit(solution)/shard_map/ppermute | solution.py:14
  257.9 8.6 %collective-permute-start.9 = (bf16[128,512]{1,0:T(8,128)(2,1)S(1)}, bf16[128,512]{1,0:T(8,128)(2,1)S(1)}, u32[]{:S(2)}, u32[]{:S(2)}) collective-permute-start(bf16[128,512]{1,0:T(8,128)(2,1)S(1)} %collective-permute-done.8), channel_id=1, source_target_pairs={{0,30},{2,0},{4,2},{6,4},{8,6},{10,8},{12,10},{14,12},{16,14},{18,... | collective-permute-start | bytes 393224 | tf_op jit(solution)/shard_map/ppermute | solution.py:14
  266.5 8.6 %collective-permute-start.10 = (bf16[128,512]{1,0:T(8,128)(2,1)S(1)}, bf16[128,512]{1,0:T(8,128)(2,1)S(1)}, u32[]{:S(2)}, u32[]{:S(2)}) collective-permute-start(bf16[128,512]{1,0:T(8,128)(2,1)S(1)} %collective-permute-done.9), channel_id=1, source_target_pairs={{0,30},{2,0},{4,2},{6,4},{8,6},{10,8},{12,10},{14,12},{16,14},{18,... | collective-permute-start | bytes 393224 | tf_op jit(solution)/shard_map/ppermute | solution.py:14
  275.1 9.1 %collective-permute-start.11 = (bf16[128,512]{1,0:T(8,128)(2,1)S(1)}, bf16[128,512]{1,0:T(8,128)(2,1)S(1)}, u32[]{:S(2)}, u32[]{:S(2)}) collective-permute-start(bf16[128,512]{1,0:T(8,128)(2,1)S(1)} %collective-permute-done.10), channel_id=1, source_target_pairs={{0,30},{2,0},{4,2},{6,4},{8,6},{10,8},{12,10},{14,12},{16,14},{18,... | collective-permute-start | bytes 393224 | tf_op jit(solution)/shard_map/ppermute | solution.py:14
  284.2 9.7 %collective-permute-start.12 = (bf16[128,512]{1,0:T(8,128)(2,1)S(1)}, bf16[128,512]{1,0:T(8,128)(2,1)S(1)}, u32[]{:S(2)}, u32[]{:S(2)}) collective-permute-start(bf16[128,512]{1,0:T(8,128)(2,1)S(1)} %collective-permute-done.11), channel_id=1, source_target_pairs={{0,30},{2,0},{4,2},{6,4},{8,6},{10,8},{12,10},{14,12},{16,14},{18,... | collective-permute-start | bytes 393224 | tf_op jit(solution)/shard_map/ppermute | solution.py:14
  293.8 8.6 %collective-permute-start.13 = (bf16[128,512]{1,0:T(8,128)(2,1)S(1)}, bf16[128,512]{1,0:T(8,128)(2,1)S(1)}, u32[]{:S(2)}, u32[]{:S(2)}) collective-permute-start(bf16[128,512]{1,0:T(8,128)(2,1)S(1)} %collective-permute-done.12), channel_id=1, source_target_pairs={{0,30},{2,0},{4,2},{6,4},{8,6},{10,8},{12,10},{14,12},{16,14},{18,... | collective-permute-start | bytes 393224 | tf_op jit(solution)/shard_map/ppermute | solution.py:14
  302.4 8.6 %collective-permute-start.14 = (bf16[128,512]{1,0:T(8,128)(2,1)S(1)}, bf16[128,512]{1,0:T(8,128)(2,1)S(1)}, u32[]{:S(2)}, u32[]{:S(2)}) collective-permute-start(bf16[128,512]{1,0:T(8,128)(2,1)S(1)} %collective-permute-done.13), channel_id=1, source_target_pairs={{0,30},{2,0},{4,2},{6,4},{8,6},{10,8},{12,10},{14,12},{16,14},{18,... | collective-permute-start | bytes 393224 | tf_op jit(solution)/shard_map/ppermute | solution.py:14
Sparse Core Ops, SparseCore 0:
  52.4 127.3 all-reduce.1
  312.4 9.7 reduce-scatter.1
